TPU v7x, 32 devices: a whole 2x2x4 slice. The times are simulated.
32 devices in a mesh: gx: 4 (over z), gy: 2 (over y), gz: 4 (over x, core).
Axes of the slice: x: 2, y: 2, z: 4, core: 2. Of those that a mesh axis runs over, the one named last changes fastest.
Arguments:
- features: bfloat16 [32, 16, 8, 512], P(None, 'gx', 'gy', 'gz'), may hold values from -6 to 6
- cotangent: bfloat16 [32, 16, 8, 512], P(None, 'gx', 'gy', 'gz'), may hold values from -6 to 6
- w_fine_in: bfloat16 [27, 32, 32], replicated, may hold values from -0.21875 to 0.21875
- w_coarse_in: bfloat16 [27, 32, 128], replicated, may hold values from -0.21875 to 0.21875
- w_coarse_mid: bfloat16 [27, 128, 128], replicated, may hold values from -0.109375 to 0.109375
- w_lift: bfloat16 [128, 32], replicated, may hold values from -0.5 to 0.5
- w_fine_out: bfloat16 [27, 32, 32], replicated, may hold values from -0.21875 to 0.21875
Outputs:
- output: bfloat16 [32, 16, 8, 512], P(None, 'gx', 'gy', 'gz')
- grad_input: bfloat16 [32, 16, 8, 512], P(None, 'gx', 'gy', 'gz')
- grad_fine_in: float32 [27, 32, 32], P(None, 'gx', ('gy', 'gz'))
- grad_coarse_in: float32 [27, 32, 128], P(None, 'gx', ('gy', 'gz'))
- grad_coarse_mid: float32 [27, 128, 128], P(None, 'gx', ('gy', 'gz'))
- grad_lift: float32 [128, 32], P('gx', ('gy', 'gz'))
- grad_fine_out: float32 [27, 32, 32], P(None, 'gx', ('gy', 'gz'))
All inputs are finite; a program needn't handle non-finite values.
Results may differ from a plain program's by a relative error of at most 0.02.
Values may be sent and summed in bfloat16 or wider, within the bound.
A program may use at most 128 MiB of HBM per device.

v0:
```python
import math

import jax
import jax.numpy as jnp
from jax import lax
from jax.experimental import pallas as pl
from jax.experimental.pallas import tpu as pltpu
from jax.sharding import PartitionSpec as P

AXES = ("gx", "gy", "gz")
MESH = pl.DeviceIdType.MESH
DIRECT = 64


def place(flat, counts):
    nx, ny, nz = counts
    return (flat // (ny * nz), (flat // nz) % ny, flat % nz)


def meet(counts, total, me):
    barrier = pltpu.get_barrier_semaphore()

    def greet(k, carry):
        pl.semaphore_signal(
            barrier, inc=1, device_id=place((me + k) % total, counts), device_id_type=MESH
        )
        return carry

    lax.fori_loop(1, total, greet, 0)
    pl.semaphore_wait(barrier, total - 1)


def spread_kernel(counts, each, x_ref, o_ref, local_sem, send_sem, recv_sem):
    total = counts[0] * counts[1] * counts[2]
    me = (lax.axis_index("gx") * counts[1] + lax.axis_index("gy")) * counts[2] + lax.axis_index(
        "gz"
    )
    meet(counts, total, me)

    def copy(k):
        peer = (me + k) % total
        return pltpu.make_async_remote_copy(
            src_ref=x_ref.at[peer] if each else x_ref,
            dst_ref=o_ref.at[me],
            send_sem=send_sem.at[k],
            recv_sem=recv_sem.at[k],
            device_id=place(peer, counts),
            device_id_type=MESH,
        )

    def begin(k, carry):
        copy(k).start()
        return carry

    def finish(k, carry):
        copy(k).wait()
        return carry

    lax.fori_loop(1, total, begin, 0)
    own = pltpu.make_async_copy(x_ref.at[me] if each else x_ref, o_ref.at[me], local_sem)
    own.start()
    own.wait()
    lax.fori_loop(1, total, finish, 0)


def spread(x, counts, each, ident):
    total = counts[0] * counts[1] * counts[2]
    block = x.shape[1:] if each else x.shape
    return pl.pallas_call(
        lambda *refs: spread_kernel(counts, each, *refs),
        out_shape=jax.ShapeDtypeStruct((total,) + block, x.dtype),
        in_specs=[pl.BlockSpec(memory_space=pltpu.VMEM)],
        out_specs=pl.BlockSpec(memory_space=pltpu.VMEM),
        scratch_shapes=[
            pltpu.SemaphoreType.DMA,
            pltpu.SemaphoreType.DMA((total,)),
            pltpu.SemaphoreType.DMA((total,)),
        ],
        compiler_params=pltpu.CompilerParams(collective_id=ident, has_side_effects=True),
        name="spread_each" if each else "spread_all",
    )(x)


def extended(cells, sides, width):
    for axis, dim in sides:
        count = lax.axis_size(axis)
        ends = count - 1
        head = lax.slice_in_dim(cells, 0, width, axis=dim)
        tail = lax.slice_in_dim(cells, cells.shape[dim] - width, cells.shape[dim], axis=dim)
        cells = jnp.concatenate(
            [
                lax.ppermute(tail, axis, [(i, (i + 1) % count) for i in range(ends)]),
                cells,
                lax.ppermute(head, axis, [((i + 1) % count, i) for i in range(ends)]),
            ],
            axis=dim,
        )
    return cells


def silu_slope(values):
    sigma = jax.nn.sigmoid(values)
    return sigma * (1.0 + values * (1.0 - sigma))


def conv_valid(padded, weight, form="NCDHW"):
    kernel = weight.reshape(3, 3, 3, weight.shape[1], weight.shape[2])
    result = lax.conv_general_dilated(
        padded[None],
        kernel,
        (1, 1, 1),
        "VALID",
        dimension_numbers=(form, "DHWIO", form),
        preferred_element_type=jnp.float32,
    )
    return result[0]


def flipped(weight):
    return jnp.flip(weight, 0).transpose(0, 2, 1)


def pool_blocks(field):
    chans, depth, height, length = field.shape
    grouped = field.astype(jnp.float32).reshape(
        chans, depth // 4, 4, height // 4, 4, length // 4, 4
    )
    return grouped.sum(axis=(2, 4, 6))


def spread_up(field):
    chans, depth, height, length = field.shape
    grown = jnp.broadcast_to(
        field[:, :, None, :, None, :, None], (chans, depth, 4, height, 4, length, 4)
    )
    return grown.reshape(chans, depth * 4, height * 4, length * 4)


def tap_grad_direct(padded, grad):
    depth = padded.shape[1] - 2
    height = padded.shape[2] - 2
    length = padded.shape[3] - 2
    flat_grad = grad.reshape(grad.shape[0], -1)
    blocks = []
    for tap in range(27):
        shift_x, shift_y, shift_z = (tap // 9, tap // 3 % 3, tap % 3)
        window = padded[
            :, shift_x : shift_x + depth, shift_y : shift_y + height, shift_z : shift_z + length
        ].reshape(padded.shape[0], -1)
        blocks.append(
            lax.dot_general(
                window, flat_grad, (((1,), (1,)), ((), ())), preferred_element_type=jnp.float32
            )
        )
    return jnp.stack(blocks)


def fine_rim(field):
    return extended(field, (("gx", 1), ("gy", 2), ("gz", 3)), 1)


def coarse_rim(field):
    return extended(field, (("gx", 1), ("gy", 2), ("gz", 3)), 1)


def reduce_grad(partial_value):
    first = lax.psum_scatter(partial_value, "gx", scatter_dimension=1, tiled=True)
    return lax.psum_scatter(first, ("gy", "gz"), scatter_dimension=2, tiled=True)


def input_share(field):
    parts = lax.all_to_all(field[None], "gx", split_axis=1, concat_axis=0, tiled=True)
    moved = jnp.moveaxis(parts, 0, 1)
    moved = moved.reshape(moved.shape[0], -1, moved.shape[3], moved.shape[4])
    moved = lax.all_gather(moved, "gy", axis=2, tiled=True)
    return lax.all_gather(moved, "gz", axis=3, tiled=True)


def output_share(field):
    parts = lax.all_to_all(field[None], ("gy", "gz"), split_axis=1, concat_axis=0, tiled=True)
    count_y = lax.axis_size("gy")
    count_z = lax.axis_size("gz")
    chans = parts.shape[1]
    depth, height, length = (parts.shape[2], parts.shape[3], parts.shape[4])
    grid = parts.reshape(count_y, count_z, chans, depth, height, length).transpose(2, 3, 0, 4, 1, 5)
    grid = grid.reshape(chans, depth, count_y * height, count_z * length)
    return lax.all_gather(grid, "gx", axis=1, tiled=True)


def shards_layered(features, cotangent, w_fine_in, w_coarse_in, w_coarse_mid, w_lift, w_fine_out):
    depth, height, length = (features.shape[1], features.shape[2], features.shape[3])
    whole_cells = (
        depth * lax.axis_size("gx") * height * lax.axis_size("gy") * length * lax.axis_size("gz")
    )
    scale = 1.0 / math.sqrt(whole_cells)
    padded_in = fine_rim(features)
    z_first = conv_valid(padded_in, w_fine_in)
    act_first = jax.nn.silu(z_first).astype(jnp.bfloat16)
    pooled = (pool_blocks(act_first) / 64.0).astype(jnp.bfloat16)
    pooled_pad = coarse_rim(pooled)
    z_second = conv_valid(pooled_pad, w_coarse_in)
    act_second = jax.nn.silu(z_second).astype(jnp.bfloat16)
    second_pad = coarse_rim(act_second)
    z_third = conv_valid(second_pad, w_coarse_mid)
    act_third = jax.nn.silu(z_third).astype(jnp.bfloat16)
    lifted = lax.dot_general(
        w_lift, act_third, (((0,), (0,)), ((), ())), preferred_element_type=jnp.float32
    )
    joined = (act_first.astype(jnp.float32) + spread_up(lifted)).astype(jnp.bfloat16)
    padded_joined = fine_rim(joined)
    output = conv_valid(padded_joined, w_fine_out).astype(jnp.bfloat16)
    part_fine_out = tap_grad_direct(padded_joined, cotangent) * scale
    d_joined = conv_valid(fine_rim(cotangent), flipped(w_fine_out))
    d_lift = pool_blocks(d_joined)
    lift_partial = (
        lax.dot_general(
            act_third.astype(jnp.float32),
            d_lift,
            (((1, 2, 3), (1, 2, 3)), ((), ())),
            precision=lax.Precision.HIGHEST,
        )
        * scale
    )
    d_third = lax.dot_general(
        w_lift.astype(jnp.float32),
        d_lift,
        (((1,), (0,)), ((), ())),
        precision=lax.Precision.HIGHEST,
    )
    dz_third = (d_third * silu_slope(z_third)).astype(jnp.bfloat16)
    dz_third_pad = coarse_rim(dz_third)
    grad_coarse_mid = None
    sources = input_share(act_second)
    sources_pad = jnp.pad(sources, ((0, 0), (1, 1), (1, 1), (1, 1)))
    targets = output_share(dz_third)
    grad_coarse_mid = tap_grad_direct(sources_pad, targets) * scale
    dz_second = (conv_valid(dz_third_pad, flipped(w_coarse_mid)) * silu_slope(z_second)).astype(
        jnp.bfloat16
    )
    dz_second_pad = coarse_rim(dz_second)
    part_coarse_in = tap_grad_direct(pooled_pad, dz_second) * scale
    d_pool = conv_valid(dz_second_pad, flipped(w_coarse_in))
    dz_first = ((d_joined + spread_up(d_pool) / 64.0) * silu_slope(z_first)).astype(jnp.bfloat16)
    part_fine_in = tap_grad_direct(padded_in, dz_first) * scale
    grad_input = conv_valid(fine_rim(dz_first), flipped(w_fine_in)).astype(jnp.bfloat16)
    pending = [part_fine_out, lift_partial[None], part_coarse_in, part_fine_in]
    reduced = [reduce_grad(partial_value) for partial_value in pending]
    grad_fine_out = reduced[0]
    grad_lift = reduced[1][0]
    grad_coarse_in = reduced[2]
    grad_fine_in = reduced[3]
    return (
        output,
        grad_input,
        grad_fine_in,
        grad_coarse_in,
        grad_coarse_mid,
        grad_lift,
        grad_fine_out,
    )


def halo_kernel(counts, x_ref, o_ref, rows, packed, from_low, from_high, sends, recvs):
    nx, ny, nz = counts
    gx, gy, gz = (lax.axis_index(axis) for axis in AXES)
    sides = [(i, j, 0) for i in (-1, 0, 1) for j in (-1, 0, 1) if (i, j) != (0, 0)]
    sides += [(0, 0, -1), (0, 0, 1)]

    def there(side, sign):
        x, y, z = gx + sign * side[0], gy + sign * side[1], gz + sign * side[2]
        real = (x >= 0) & (x < nx) & (y >= 0) & (y < ny) & (z >= 0) & (z < nz)
        return (x, y, z), real

    rows[...] = jnp.zeros_like(rows)
    from_low[...] = jnp.zeros_like(from_low)
    from_high[...] = jnp.zeros_like(from_high)
    barrier = pltpu.get_barrier_semaphore()
    met = 0
    for side in sides:
        peer, real = there(side, 1)
        met = met + jnp.where(real, 1, 0)

        @pl.when(real)
        def _():
            pl.semaphore_signal(barrier, inc=1, device_id=peer, device_id_type=MESH)

    pl.semaphore_wait(barrier, met)
    d, h = x_ref.shape[:2]
    take = {-1: lambda n: pl.ds(0, 2), 0: lambda n: pl.ds(0, n), 1: lambda n: pl.ds(n - 2, 2)}
    land = {-1: lambda n: pl.ds(n + 2, 2), 0: lambda n: pl.ds(2, n), 1: lambda n: pl.ds(0, 2)}

    def transfer(k, side):
        if k < 8:
            source = x_ref.at[take[side[0]](d), take[side[1]](h)]
            target = rows.at[land[side[0]](d), land[side[1]](h)]
        else:
            source, target = packed, (from_high if side[2] < 0 else from_low)
        return pltpu.make_async_remote_copy(
            src_ref=source,
            dst_ref=target,
            send_sem=sends.at[k],
            recv_sem=recvs.at[k],
            device_id=there(side, 1)[0],
            device_id_type=MESH,
        )

    def run(first, last):
        for k in range(first, last):

            @pl.when(there(sides[k], 1)[1])
            def _():
                transfer(k, sides[k]).start()

    def settle(first, last):
        for k in range(first, last):

            @pl.when(there(sides[k], -1)[1])
            def _():
                transfer(k, sides[k]).wait_recv()

            @pl.when(there(sides[k], 1)[1])
            def _():
                transfer(k, sides[k]).wait_send()

    run(0, 8)
    settle(0, 8)
    rows[2 : 2 + d, 2 : 2 + h] = x_ref[...]
    lane = lax.broadcasted_iota(jnp.int32, (x_ref.shape[2], 128), 1)
    spots = [(x, y) for x in range(d + 4) for y in range(h + 4)]
    for part in range(2):
        group = jnp.zeros(lane.shape, jnp.float32)
        for r in range(32):
            x, y = spots[part * 32 + r]
            turned = pltpu.roll(rows[x, y].astype(jnp.float32), (2 + 4 * r) % 128, 1)
            group = jnp.where(lane // 4 == r, turned, group)
        packed[:, part * 128 : part * 128 + 128] = group.astype(jnp.bfloat16)
    run(8, 10)
    for x, y in spots:
        o_ref[x, y, :, 0:128] = rows[x, y]
    settle(8, 10)
    for part in range(2):
        span = slice(part * 128, part * 128 + 128)
        group = jnp.where(
            lane % 4 >= 2,
            from_high[:, span].astype(jnp.float32),
            from_low[:, span].astype(jnp.float32),
        )
        for r in range(32):
            x, y = spots[part * 32 + r]
            o_ref[x, y, :, 128:256] = pltpu.roll(group, 126 - 4 * r if r < 32 else 0, 1).astype(
                jnp.bfloat16
            )


def vmem(count):
    return [pl.BlockSpec(memory_space=pltpu.VMEM)] * count


ROOMY = 60 * 1024 * 1024


def halo(x, counts, ident):
    d, h, chans, length = x.shape
    edge = pltpu.VMEM((chans, 256), jnp.bfloat16)
    return pl.pallas_call(
        lambda *refs: halo_kernel(counts, *refs),
        out_shape=jax.ShapeDtypeStruct((d + 4, h + 4, chans, 256), x.dtype),
        in_specs=vmem(1),
        out_specs=vmem(1)[0],
        scratch_shapes=[
            pltpu.VMEM((d + 4, h + 4, chans, length), x.dtype),
            edge,
            edge,
            edge,
            pltpu.SemaphoreType.DMA((10,)),
            pltpu.SemaphoreType.DMA((10,)),
        ],
        compiler_params=pltpu.CompilerParams(
            collective_id=ident, has_side_effects=True, vmem_limit_bytes=ROOMY
        ),
        name="halo",
    )(x)


def stacked(value):
    size = value.shape[1]
    return jnp.concatenate(
        [pltpu.roll(value, 1, 1), value, pltpu.roll(value, size - 1, 1)]
    ).astype(jnp.bfloat16)


def around(ref, x, y, rows, lanes):
    return jnp.concatenate(
        [ref[x + a, y + b, rows, lanes] for a in range(3) for b in range(3)]
    )


def dot(a, b):
    return jnp.dot(a, b, preferred_element_type=jnp.float32)


def dot_over(a, b, dims, precision=None):
    return lax.dot_general(
        a, b, ((dims[:1], dims[1:]), ((), ())), precision=precision, preferred_element_type=jnp.float32
    )


def fine_kernel(ext, w_in, w_out_back, z_ref, d_ref, mine, taps, total):
    def fill(r, carry):
        x, y = r // 8, r % 8
        for f in range(2):
            value = ext[x, y, f * 32 : f * 32 + 32, :].astype(jnp.float32)
            taps[x, y, f * 96 : f * 96 + 96, :] = stacked(value)
        return carry

    lax.fori_loop(0, 64, fill, 0)
    total[...] = jnp.zeros_like(total)

    def body(r, carry):
        x, y = r // 6, r % 6
        z = dot(w_in[...], around(taps, x, y, slice(0, 96), slice(None)))
        d = dot(w_out_back[...], around(taps, x, y, slice(96, 192), slice(None)))
        z_ref[x, y] = z
        d_ref[x, y] = d
        act = jax.nn.silu(z[:, :128]).astype(jnp.bfloat16).astype(jnp.float32)
        own = jnp.where((x >= 1) & (x <= 4) & (y >= 1) & (y <= 4), 1.0, 0.0)
        total[...] += own * jnp.concatenate([act, d[:, :128]])
        return carry

    lax.fori_loop(0, 36, body, 0)
    row = lax.broadcasted_iota(jnp.int32, (32, 128), 0)
    lane = lax.broadcasted_iota(jnp.int32, (32, 128), 1)
    pick = jnp.where(lane // 4 == row, 1.0, 0.0)
    sums = dot_over(pick, total[...], (1, 1), lax.Precision.HIGHEST)
    both = jnp.concatenate([sums[:, :32] * (1.0 / 64.0), sums[:, 32:]], axis=1)
    mine[...] = jnp.concatenate([both[:16], both[16:]], axis=1).astype(jnp.bfloat16)


def coarse_kernel(
    counts, scale, full, w_in, w_mid, w_lift, w_lift_back, w_mid_back, w_in_back,
    pick_mid, pick_in, pick_o, pick_lift,
    grown, g_mid, g_in, g_lift,
    pad_in, pad_mid, pad_smid, pad_sin, table,
):
    nx, ny, nz = counts
    cells = nx * ny * 128
    gx, gy, gz = (lax.axis_index(axis) for axis in AXES)
    for pad in (pad_in, pad_mid, pad_smid, pad_sin):
        pad[...] = jnp.zeros_like(pad)

    def fill(pad, value):
        at = lax.broadcasted_iota(jnp.int32, value.shape, 0) % 128
        low = jnp.where(at == 0, 0.0, pltpu.roll(value, 1, 0))
        high = jnp.where(at == 127, 0.0, pltpu.roll(value, cells - 1, 0))
        wide = jnp.concatenate([low, value, high], axis=1).astype(jnp.bfloat16)
        pad[1 : nx + 1, 1 : ny + 1] = wide.reshape(nx, ny, 128, wide.shape[1])

    def window(pad, ab):
        a, b = ab // 3, ab % 3
        return pad[a : a + nx, b : b + ny].reshape(cells, pad.shape[3])

    def conv(pad, weight):
        result = dot(window(pad, 0), weight[0])
        for ab in range(1, 9):
            result = result + dot(window(pad, ab), weight[ab])
        return result

    def slope(v):
        sigma = jax.nn.sigmoid(v)
        return sigma * (1.0 + v * (1.0 - sigma))

    pieces = []
    for k in range(nx * ny):
        for z in range(nz):
            block = full[k * nz + z]
            pieces += [block[:, :64], block[:, 64:]]
    both = jnp.concatenate(pieces)
    pooled, d_lift = both[:, :32], both[:, 32:]
    fill(pad_in, pooled.astype(jnp.float32))
    z_second = conv(pad_in, w_in)
    act_second = jax.nn.silu(z_second)
    fill(pad_mid, act_second)
    z_third = conv(pad_mid, w_mid)
    act_third = jax.nn.silu(z_third).astype(jnp.bfloat16)
    lifted = dot(act_third, w_lift[...])
    dz_third = (dot(d_lift, w_lift_back[...]) * slope(z_third)).astype(jnp.bfloat16)
    fill(pad_mid, dz_third.astype(jnp.float32))
    dz_second = (conv(pad_mid, w_mid_back) * slope(z_second)).astype(jnp.bfloat16)
    fill(pad_mid, dz_second.astype(jnp.float32))
    d_pool = conv(pad_mid, w_in_back)

    table[...] = (
        jnp.concatenate([lifted, d_pool * (1.0 / 64.0)], axis=1)
        .astype(jnp.bfloat16)
        .reshape(nx, ny, 128, 64)
    )
    row = lax.broadcasted_iota(jnp.int32, (128, 256), 0)
    lane = lax.broadcasted_iota(jnp.int32, (128, 256), 1)
    cell = jnp.where(lane < 192, lane // 4, -1) + gz * 32
    grow = jnp.where(row == cell, 1.0, 0.0).astype(jnp.bfloat16)
    for i in range(3):
        for j in range(3):
            x = jnp.clip(gx + i - 1, 0, nx - 1)
            y = jnp.clip(gy + j - 1, 0, ny - 1)
            grown[i, j] = dot_over(table[x, y], grow, (0, 0))

    third_o = dot(dz_third, pick_o[...]).T.astype(jnp.bfloat16)
    second_o = dot(dz_second, pick_o[...]).T.astype(jnp.bfloat16)
    fill(pad_smid, dot(act_second.astype(jnp.bfloat16), pick_mid[...]))
    fill(pad_sin, dot(pooled, pick_in[...]))
    for ab in range(9):
        g_mid[ab] = dot(third_o, window(pad_smid, ab)) * scale
        g_in[ab] = dot(second_o, window(pad_sin, ab)) * scale
    third_i = dot(act_third, pick_mid[...]).astype(jnp.bfloat16)
    lift_o = dot(d_lift, pick_lift[...]).T.astype(jnp.bfloat16)
    g_lift[...] = dot(lift_o, third_i) * scale


def last_kernel(
    counts, ext, z_ref, d_ref, grown, w_out, w_in_back, out, g_input, parts, tj, td, tf, sums
):
    nx, ny, nz = counts
    gx, gy, gz = (lax.axis_index(axis) for axis in AXES)
    lane = lax.broadcasted_iota(jnp.int32, (32, 256), 1)
    at_z = gz * 128 + jnp.where(lane < 192, lane, lane - 256)
    keep_z = jnp.where((at_z >= 0) & (at_z < nz * 128), 1.0, 0.0)

    def fill(r, carry):
        x, y = r // 6, r % 6
        at_x, at_y = gx * 4 + x - 1, gy * 4 + y - 1
        real = (at_x >= 0) & (at_x < nx * 4) & (at_y >= 0) & (at_y < ny * 4)
        keep = keep_z * jnp.where(real, 1.0, 0.0)
        up = grown[(x + 3) // 4, (y + 3) // 4]
        z = z_ref[x, y]
        sigma = jax.nn.sigmoid(z)
        act = (z * sigma).astype(jnp.bfloat16).astype(jnp.float32)
        joined = (act + up[:32]).astype(jnp.bfloat16).astype(jnp.float32) * keep
        dz = (d_ref[x, y] + up[32:]) * (sigma * (1.0 + z * (1.0 - sigma))) * keep
        dz = dz.astype(jnp.bfloat16).astype(jnp.float32)
        tj[x, y] = stacked(joined)[:, :128]
        td[x, y] = stacked(dz)[:, :128]
        tf[x, y] = stacked(ext[x + 1, y + 1, 0:32, :].astype(jnp.float32))[:, :128]
        return carry

    lax.fori_loop(0, 36, fill, 0)
    sums[...] = jnp.zeros_like(sums)

    def body(r, carry):
        x, y = r // 2, (r % 2) * 2
        whole = slice(None)

        def pair(ref):
            return jnp.concatenate(
                [around(ref, x, y, whole, whole), around(ref, x, y + 1, whole, whole)], axis=1
            )

        near = pair(tj)
        result = dot(w_out[...], near).astype(jnp.bfloat16)
        out[x, y], out[x, y + 1] = result[:, :128], result[:, 128:]
        cot = jnp.concatenate(
            [ext[x + 2, y + 2, 32:64, 0:128], ext[x + 2, y + 3, 32:64, 0:128]], axis=1
        )
        sums[0] += dot_over(near, cot, (1, 1))
        result = dot(w_in_back[...], pair(td)).astype(jnp.bfloat16)
        g_input[x, y], g_input[x, y + 1] = result[:, :128], result[:, 128:]
        grad = jnp.concatenate(
            [td[x + 1, y + 1, 32:64, :], td[x + 1, y + 2, 32:64, :]], axis=1
        )
        sums[1] += dot_over(pair(tf), grad, (1, 1))
        return carry

    lax.fori_loop(0, 8, body, 0)
    ci, co = 32 // nx, 32 // (ny * nz)
    for f in range(2):
        value = sums[f].reshape(27, nx, ci, 32)
        for i in range(nx):
            block = value[:, i].reshape(27 * ci, 32).T
            for j in range(ny * nz):
                parts[i * ny * nz + j, f * co : f * co + co, 0 : 27 * ci] = block[
                    j * co : j * co + co
                ].astype(jnp.bfloat16)


def shards(features, cotangent, w_fine_in, w_coarse_in, w_coarse_mid, w_lift, w_fine_out):
    counts = tuple(lax.axis_size(axis) for axis in AXES)
    nx, ny, nz = counts
    total = nx * ny * nz
    at_x, at_y, at_z = (lax.axis_index(axis) for axis in AXES)
    chans, depth, height, length = features.shape
    wide = w_lift.shape[0]
    scale = 1.0 / math.sqrt(total * depth * height * length)
    f32, bf16 = jnp.float32, jnp.bfloat16
    shape = jax.ShapeDtypeStruct
    params = pltpu.CompilerParams(vmem_limit_bytes=ROOMY)

    def ahead(weight):
        return weight.transpose(2, 0, 1).reshape(weight.shape[2], -1)

    def back(weight):
        return jnp.flip(weight, 0).transpose(1, 0, 2).reshape(weight.shape[1], -1)

    rows = jnp.concatenate([features, cotangent]).transpose(1, 2, 0, 3)
    ext = halo(rows, counts, 2)
    field = shape((6, 6, chans, 256), f32)
    z_first, d_joined, mine = pl.pallas_call(
        fine_kernel,
        out_shape=(field, field, shape((16, 128), bf16)),
        in_specs=vmem(3),
        out_specs=vmem(3),
        scratch_shapes=[pltpu.VMEM((8, 8, 192, 256), bf16), pltpu.VMEM((64, 128), f32)],
        compiler_params=params,
        name="fine",
    )(ext, ahead(w_fine_in), back(w_fine_out))

    full = spread(mine, counts, False, 0)

    def pick(size, parts, index):
        each = size // parts
        return (jnp.arange(size)[:, None] == index * each + jnp.arange(each)).astype(bf16)

    at_o = at_y * nz + at_z
    co, cw = wide // (ny * nz), wide // nx
    ci = chans // nx
    pads = [3 * chans, 3 * wide, 3 * cw, 3 * ci]
    grown, g_mid, g_in, g_lift = pl.pallas_call(
        lambda *refs: coarse_kernel(counts, scale, *refs),
        out_shape=(
            shape((3, 3, 2 * chans, 256), f32),
            shape((9, co, 3 * cw), f32),
            shape((9, co, 3 * ci), f32),
            shape((chans // (ny * nz), cw), f32),
        ),
        in_specs=vmem(11),
        out_specs=vmem(4),
        scratch_shapes=[pltpu.VMEM((nx + 2, ny + 2, 128, k), bf16) for k in pads]
        + [pltpu.VMEM((nx, ny, 128, 2 * chans), bf16)],
        compiler_params=params,
        name="coarse",
    )(
        full,
        w_coarse_in.reshape(9, 3 * chans, wide),
        w_coarse_mid.reshape(9, 3 * wide, wide),
        w_lift,
        w_lift.T,
        flipped(w_coarse_mid).reshape(9, 3 * wide, wide),
        flipped(w_coarse_in).reshape(9, 3 * wide, chans),
        pick(wide, nx, at_x),
        pick(chans, nx, at_x),
        pick(wide, ny * nz, at_o),
        pick(chans, ny * nz, at_o),
    )

    near = pltpu.VMEM((6, 6, 3 * chans, 128), bf16)
    block = (2 * chans // (ny * nz), 27 * ci)
    output, grad_input, parts = pl.pallas_call(
        lambda *refs: last_kernel(counts, *refs),
        out_shape=(
            shape((4, 4, chans, 128), bf16),
            shape((4, 4, chans, 128), bf16),
            shape((total,) + block, bf16),
        ),
        in_specs=vmem(6),
        out_specs=vmem(3),
        scratch_shapes=[near, near, near, pltpu.VMEM((2, 27 * chans, chans), f32)],
        compiler_params=params,
        name="last",
    )(ext, z_first, d_joined, grown, ahead(w_fine_out), back(w_fine_in))

    sums = spread(parts, counts, True, 1).astype(f32).sum(0) * scale
    sums = sums.reshape(2, -1, 27, ci).transpose(0, 2, 3, 1)

    def owned(grad):
        return grad.reshape(9, grad.shape[1], 3, -1).transpose(0, 2, 3, 1).reshape(
            27, -1, grad.shape[1]
        )

    return (
        output.transpose(2, 0, 1, 3),
        grad_input.transpose(2, 0, 1, 3),
        sums[1],
        owned(g_in),
        owned(g_mid),
        g_lift.T,
        sums[0],
    )


def choose(features, *rest):
    nx, ny, nz = (lax.axis_size(axis) for axis in AXES)
    total = nx * ny * nz
    wide = rest[4].shape[0]
    fits = features.shape == (32, 4, 4, 128) and nz == 4 and total <= DIRECT
    fits = fits and 32 % (ny * nz) == 0 and 32 % nx == 0 and 32 // nx == 8 and wide == 128
    return (shards if fits else shards_layered)(features, *rest)


def solution(mesh):
    whole = P(None, "gx", "gy", "gz")
    split = P(None, "gx", ("gy", "gz"))
    return jax.shard_map(
        choose,
        mesh=mesh,
        in_specs=(whole, whole, P(), P(), P(), P(), P()),
        out_specs=(whole, whole, split, split, split, P("gx", ("gy", "gz")), split),
        check_vma=False,
    )
```

profile of v0, /device:TPU:0, one launch (start us, length us, event | category | flops | bytes accessed | tf_op | source)
XLA Modules:
  0.0 101.8 jit_solution(11232501866815802398)
XLA Ops:
  0.6 0.9 copy.43
  1.6 0.9 copy.42
  2.5 0.7 maximum_bitcast_fusion.refs_0_
  3.3 13.9 %halo.1.ext.refs_0_ = bf16[8,8,64,256]{3,2,1,0:T(8,128)(2,1)} custom-call(bf16[4,4,64,128]{3,2,1,0:T(8,128)(2,1)} %maximum_bitcast_fusion.refs_0_), custom_call_target="tpu_custom_call" | custom-call | tf_op jit(solution)/shard_map/halo/pallas_call | solution.py:365
  17.2 0.7 copy.58.w_in
  18.0 0.1 copy.45
  18.1 0.9 reshape.71.w_out_back
  19.0 19.2 %fine.1 = (f32[6,6,32,256]{3,2,1,0:T(8,128)}, f32[6,6,32,256]{3,2,1,0:T(8,128)}, bf16[16,128]{1,0:T(8,128)(2,1)}) custom-call(bf16[8,8,64,256]{3,2,1,0:T(8,128)(2,1)} %halo.1.ext.refs_0_, bf16[32,864]{1,0:T(8,128)(2,1)} %copy.58.w_in, bf16[32,864]{1,0:T(8,128)(2,1)} %reshape.71.w_out_back), custom_call_target="tpu_custom_call" | custom-call | tf_op jit(solution)/shard_map/fine/pallas_call | solution.py:605
  38.2 12.5 %spread_all.1.refs_0_ = bf16[32,16,128]{2,1,0:T(8,128)(2,1)} custom-call(bf16[16,128]{1,0:T(8,128)(2,1)} %get-tuple-element.19.refs_0_), custom_call_target="tpu_custom_call" | custom-call | tf_op jit(solution)/shard_map/spread_all/pallas_call | solution.py:69
  50.7 0.7 copy.48.refs_3_
  51.5 1.6 %copy.46 = bf16[27,128,128]{2,1,0:T(8,128)(2,1)} copy(bf16[27,128,128]{1,2,0:T(8,128)(2,1)S(1)} %reverse_bitcast_fusion) | data formatting | bytes 1769472 | tf_op jit(solution)/shard_map/transpose | solution.py:120
  53.2 1.3 %copy.47 = bf16[27,128,32]{2,1,0:T(8,128)(2,1)} copy(bf16[27,128,32]{1,2,0:T(8,128)(2,1)S(1)} %reverse_bitcast_fusion.2) | data formatting | bytes 442368 | tf_op jit(solution)/shard_map/transpose | solution.py:120
  54.5 0.6 fusion.refs_7_
  55.1 0.6 fusion.2.refs_8_
  55.7 0.6 fusion.1.refs_9_
  56.4 0.6 fusion.3.refs_10_
  57.0 13.1 %coarse.1 = (f32[3,3,64,256]{3,2,1,0:T(8,128)}, f32[9,16,96]{2,1,0:T(8,128)}, f32[9,16,24]{2,1,0:T(8,128)}, f32[4,32]{1,0:T(4,128)}) custom-call(bf16[32,16,128]{2,1,0:T(8,128)(2,1)} %spread_all.1.refs_0_, bf16[9,96,128]{2,1,0:T(8,128)(2,1)} %bitcast.40, bf16[9,384,128]{2,1,0:T(8,128)(2,1)} %bitcast.36, bf16[128,32]{1,0:T(8,128)(2,1)} %copy.48.refs_3_, ...), custom_call_target="tpu_custom_call" | custom-call | tf_op jit(solution)/shard_map/coarse/pallas_call | solution.py:625
  70.1 0.7 copy.59.refs_4_
  70.9 0.1 copy.50
  71.0 0.9 reshape.77.refs_5_
  71.8 11.6 %last.1 = (bf16[4,4,32,128]{3,2,1,0:T(8,128)(2,1)}, bf16[4,4,32,128]{3,2,1,0:T(8,128)(2,1)}, bf16[32,8,216]{2,1,0:T(8,128)(2,1)}) custom-call(bf16[8,8,64,256]{3,2,1,0:T(8,128)(2,1)} %halo.1.ext.refs_0_, f32[6,6,32,256]{3,2,1,0:T(8,128)} %get-tuple-element.17.refs_1_, f32[6,6,32,256]{3,2,1,0:T(8,128)} %get-tuple-element.18.refs_2_, ...), custom_call_target="tpu_custom_call" | custom-call | tf_op jit(solution)/shard_map/last/pallas_call | solution.py:655
  83.5 1.7 %copy.53 = bf16[32,4,4,128]{3,2,1,0:T(4,128)(2,1)} copy(bf16[32,4,4,128]{3,0,2,1:T(8,128)(2,1)} %bitcast.47) | data formatting | bytes 262144
  85.2 1.6 %copy.54 = bf16[32,4,4,128]{3,2,1,0:T(4,128)(2,1)} copy(bf16[32,4,4,128]{3,0,2,1:T(8,128)(2,1)} %bitcast.46) | data formatting | bytes 262144
  86.8 10.8 %spread_each.1 = bf16[32,8,216]{2,1,0:T(8,128)(2,1)} custom-call(bf16[32,8,216]{2,1,0:T(8,128)(2,1)} %get-tuple-element.23.refs_0_), custom_call_target="tpu_custom_call" | custom-call | tf_op jit(solution)/shard_map/spread_each/pallas_call | solution.py:69
  97.6 0.9 convert_reduce_fusion
  98.6 0.1 mul.32
  98.7 0.7 copy.55
  99.4 0.1 copy.51
  99.5 0.8 copy.56
  100.3 0.2 reshape.80
  100.4 0.7 copy.52
  101.1 0.7 copy.57
  (24 shorter events, 0.2 us)
Async XLA Ops:
  3.3 14.0 %copy-start.3 = (bf16[27,32,32]{2,1,0:T(8,128)(2,1)S(1)}, bf16[27,32,32]{2,1,0:T(8,128)(2,1)}, u32[]{:S(2)}) copy-start(bf16[27,32,32]{2,1,0:T(8,128)(2,1)} %param.9) | copy-start | bytes 165892
  3.3 14.7 %copy-start.2 = (bf16[27,32,32]{2,1,0:T(8,128)(2,1)S(1)}, bf16[27,32,32]{2,1,0:T(8,128)(2,1)}, u32[]{:S(2)}) copy-start(bf16[27,32,32]{2,1,0:T(8,128)(2,1)} %param.13) | copy-start | bytes 165892
  19.0 31.7 %copy-start.6 = (bf16[128,32]{0,1:T(8,128)(2,1)S(1)}, bf16[128,32]{0,1:T(8,128)(2,1)}, u32[]{:S(2)}) copy-start(bf16[128,32]{0,1:T(8,128)(2,1)} %param.12) | copy-start | bytes 24580
  19.0 32.5 %copy-start = (bf16[27,128,128]{2,1,0:T(8,128)(2,1)S(1)}, bf16[27,128,128]{2,1,0:T(8,128)(2,1)}, u32[]{:S(2)}) copy-start(bf16[27,128,128]{2,1,0:T(8,128)(2,1)} %param.11) | copy-start | bytes 2654212
  51.5 1.7 %copy-start.1 = (bf16[27,32,128]{2,1,0:T(8,128)(2,1)S(1)}, bf16[27,32,128]{2,1,0:T(8,128)(2,1)}, u32[]{:S(2)}) copy-start(bf16[27,32,128]{2,1,0:T(8,128)(2,1)} %param.10) | copy-start | bytes 663556
  83.5 15.9 %copy-start.5 = (f32[9,16,24]{2,1,0:T(8,128)S(1)}, f32[9,16,24]{2,1,0:T(8,128)}, u32[]{:S(2)}) copy-start(f32[9,16,24]{2,1,0:T(8,128)} %get-tuple-element.24) | copy-start | bytes 41476
  83.5 16.8 %copy-start.4 = (f32[9,16,96]{2,1,0:T(8,128)S(1)}, f32[9,16,96]{2,1,0:T(8,128)}, u32[]{:S(2)}) copy-start(f32[9,16,96]{2,1,0:T(8,128)} %get-tuple-element.25) | copy-start | bytes 165892
where the time goes:
time: 102 us
  Pallas kernels  81.3 us (80%)
  local copies, waits for them, and re-layouts  15.6 us (15%)
  other arithmetic  4.16 us (4%)
    pallas_call x2, Pallas kernels, spread(): pl.pallas_call(lambda *refs: spread_kernel(counts, each, *refs), out_shap...  23.3 us
    pallas_call x1, Pallas kernels, shards(): pl.pallas_call(fine_kernel, out_shape=(field, field, shape((16, 128), bf1...  19.2 us
    pallas_call x1, Pallas kernels, halo(): pl.pallas_call(lambda *refs: halo_kernel(counts, *refs), out_shape=jax.Sh...  13.9 us
    pallas_call x1, Pallas kernels, shards(): pl.pallas_call(lambda *refs: coarse_kernel(counts, scale, *refs), out_sha...  13.1 us
    pallas_call x1, Pallas kernels, shards(): pl.pallas_call(lambda *refs: last_kernel(counts, *refs), out_shape=(shape...  11.6 us
    unnamed x22, local copies, waits for them, and re-layouts  8.08 us
    transpose x4, local copies, waits for them, and re-layouts, flipped(): return jnp.flip(weight, 0).transpose(0, 2, 1)  3.03 us
    convert_element_type x4, other arithmetic, pick(): (jnp.arange(size)[:, None] == index * each + jnp.arange(each)).astype(bf16)  2.47 us

commit v1 on v0

--- a/solution.py
+++ b/solution.py
@@ -30,7 +30,7 @@
     pl.semaphore_wait(barrier, total - 1)
 
 
-def spread_kernel(counts, each, x_ref, o_ref, local_sem, send_sem, recv_sem):
+def spread_kernel(counts, each, x_ref, o_ref, local_sem, send_sem, recv_sem, during):
     total = counts[0] * counts[1] * counts[2]
     me = (lax.axis_index("gx") * counts[1] + lax.axis_index("gy")) * counts[2] + lax.axis_index(
         "gz"
@@ -59,26 +59,48 @@
     lax.fori_loop(1, total, begin, 0)
     own = pltpu.make_async_copy(x_ref.at[me] if each else x_ref, o_ref.at[me], local_sem)
     own.start()
+    during()
     own.wait()
     lax.fori_loop(1, total, finish, 0)
 
 
-def spread(x, counts, each, ident):
+def gather_kernel(counts, x_ref, w_mid, w_in, o_ref, mid_back, in_back, *sems):
+    wide, narrow = w_mid.shape[2], in_back.shape[2]
+
+    def turn():
+        def body(ab, carry):
+            for c in range(3):
+                rows = slice(c * wide, c * wide + wide)
+                mid_back[ab, rows, :] = w_mid[8 - ab, (2 - c) * wide : (3 - c) * wide, :].T
+                in_back[ab, rows, :] = w_in[8 - ab, (2 - c) * narrow : (3 - c) * narrow, :].T
+            return carry
+
+        lax.fori_loop(0, 9, body, 0)
+
+    spread_kernel(counts, False, x_ref, o_ref, *sems, turn)
+
+
+def sum_kernel(counts, scale, x_ref, o_ref, landed, *sems):
+    spread_kernel(counts, True, x_ref, landed, *sems, lambda: None)
+    o_ref[...] = landed[...].astype(jnp.float32).sum(0) * scale
+
+
+def spread_call(kernel, counts, ident, outs, scratch, name, *args):
     total = counts[0] * counts[1] * counts[2]
-    block = x.shape[1:] if each else x.shape
     return pl.pallas_call(
-        lambda *refs: spread_kernel(counts, each, *refs),
-        out_shape=jax.ShapeDtypeStruct((total,) + block, x.dtype),
-        in_specs=[pl.BlockSpec(memory_space=pltpu.VMEM)],
-        out_specs=pl.BlockSpec(memory_space=pltpu.VMEM),
-        scratch_shapes=[
+        kernel,
+        out_shape=outs,
+        in_specs=vmem(len(args)),
+        out_specs=vmem(len(outs)),
+        scratch_shapes=scratch
+        + [
             pltpu.SemaphoreType.DMA,
             pltpu.SemaphoreType.DMA((total,)),
             pltpu.SemaphoreType.DMA((total,)),
         ],
         compiler_params=pltpu.CompilerParams(collective_id=ident, has_side_effects=True),
-        name="spread_each" if each else "spread_all",
-    )(x)
+        name=name,
+    )(*args)
 
 
 def extended(cells, sides, width):
@@ -405,7 +427,17 @@
     )
 
 
-def fine_kernel(ext, w_in, w_out_back, z_ref, d_ref, mine, taps, total):
+def ahead(weight):
+    return weight[...].reshape(27 * weight.shape[1], weight.shape[2]).T
+
+
+def back(weight):
+    return jnp.concatenate([weight[26 - t] for t in range(27)], axis=1)
+
+
+def fine_kernel(ext, w_in, w_out, z_ref, d_ref, mine, taps, total, ws):
+    ws[0], ws[1] = ahead(w_in), back(w_out)
+
     def fill(r, carry):
         x, y = r // 8, r % 8
         for f in range(2):
@@ -418,8 +450,8 @@
 
     def body(r, carry):
         x, y = r // 6, r % 6
-        z = dot(w_in[...], around(taps, x, y, slice(0, 96), slice(None)))
-        d = dot(w_out_back[...], around(taps, x, y, slice(96, 192), slice(None)))
+        z = dot(ws[0], around(taps, x, y, slice(0, 96), slice(None)))
+        d = dot(ws[1], around(taps, x, y, slice(96, 192), slice(None)))
         z_ref[x, y] = z
         d_ref[x, y] = d
         act = jax.nn.silu(z[:, :128]).astype(jnp.bfloat16).astype(jnp.float32)
@@ -437,8 +469,7 @@
 
 
 def coarse_kernel(
-    counts, scale, full, w_in, w_mid, w_lift, w_lift_back, w_mid_back, w_in_back,
-    pick_mid, pick_in, pick_o, pick_lift,
+    counts, scale, full, w_in, w_mid, w_lift, w_mid_back, w_in_back,
     grown, g_mid, g_in, g_lift,
     pad_in, pad_mid, pad_smid, pad_sin, table,
 ):
@@ -447,6 +478,16 @@
     gx, gy, gz = (lax.axis_index(axis) for axis in AXES)
     for pad in (pad_in, pad_mid, pad_smid, pad_sin):
         pad[...] = jnp.zeros_like(pad)
+
+    def pick(size, parts, index):
+        each = size // parts
+        row = lax.broadcasted_iota(jnp.int32, (size, each), 0)
+        column = lax.broadcasted_iota(jnp.int32, (size, each), 1)
+        return jnp.where(row == index * each + column, 1.0, 0.0).astype(jnp.bfloat16)
+
+    at_o = gy * nz + gz
+    pick_mid, pick_in = pick(128, nx, gx), pick(32, nx, gx)
+    pick_o, pick_lift = pick(128, ny * nz, at_o), pick(32, ny * nz, at_o)
 
     def fill(pad, value):
         at = lax.broadcasted_iota(jnp.int32, value.shape, 0) % 128
@@ -483,7 +524,7 @@
     z_third = conv(pad_mid, w_mid)
     act_third = jax.nn.silu(z_third).astype(jnp.bfloat16)
     lifted = dot(act_third, w_lift[...])
-    dz_third = (dot(d_lift, w_lift_back[...]) * slope(z_third)).astype(jnp.bfloat16)
+    dz_third = (dot_over(d_lift, w_lift[...], (1, 1)) * slope(z_third)).astype(jnp.bfloat16)
     fill(pad_mid, dz_third.astype(jnp.float32))
     dz_second = (conv(pad_mid, w_mid_back) * slope(z_second)).astype(jnp.bfloat16)
     fill(pad_mid, dz_second.astype(jnp.float32))
@@ -504,21 +545,22 @@
             y = jnp.clip(gy + j - 1, 0, ny - 1)
             grown[i, j] = dot_over(table[x, y], grow, (0, 0))
 
-    third_o = dot(dz_third, pick_o[...]).T.astype(jnp.bfloat16)
-    second_o = dot(dz_second, pick_o[...]).T.astype(jnp.bfloat16)
-    fill(pad_smid, dot(act_second.astype(jnp.bfloat16), pick_mid[...]))
-    fill(pad_sin, dot(pooled, pick_in[...]))
+    third_o = dot(dz_third, pick_o).T.astype(jnp.bfloat16)
+    second_o = dot(dz_second, pick_o).T.astype(jnp.bfloat16)
+    fill(pad_smid, dot(act_second.astype(jnp.bfloat16), pick_mid))
+    fill(pad_sin, dot(pooled, pick_in))
     for ab in range(9):
         g_mid[ab] = dot(third_o, window(pad_smid, ab)) * scale
         g_in[ab] = dot(second_o, window(pad_sin, ab)) * scale
-    third_i = dot(act_third, pick_mid[...]).astype(jnp.bfloat16)
-    lift_o = dot(d_lift, pick_lift[...]).T.astype(jnp.bfloat16)
+    third_i = dot(act_third, pick_mid).astype(jnp.bfloat16)
+    lift_o = dot(d_lift, pick_lift).T.astype(jnp.bfloat16)
     g_lift[...] = dot(lift_o, third_i) * scale
 
 
 def last_kernel(
-    counts, ext, z_ref, d_ref, grown, w_out, w_in_back, out, g_input, parts, tj, td, tf, sums
+    counts, ext, z_ref, d_ref, grown, w_out, w_in, out, g_input, parts, tj, td, tf, sums, ws
 ):
+    ws[0], ws[1] = ahead(w_out), back(w_in)
     nx, ny, nz = counts
     gx, gy, gz = (lax.axis_index(axis) for axis in AXES)
     lane = lax.broadcasted_iota(jnp.int32, (32, 256), 1)
@@ -555,13 +597,13 @@
             )
 
         near = pair(tj)
-        result = dot(w_out[...], near).astype(jnp.bfloat16)
+        result = dot(ws[0], near).astype(jnp.bfloat16)
         out[x, y], out[x, y + 1] = result[:, :128], result[:, 128:]
         cot = jnp.concatenate(
             [ext[x + 2, y + 2, 32:64, 0:128], ext[x + 2, y + 3, 32:64, 0:128]], axis=1
         )
         sums[0] += dot_over(near, cot, (1, 1))
-        result = dot(w_in_back[...], pair(td)).astype(jnp.bfloat16)
+        result = dot(ws[1], pair(td)).astype(jnp.bfloat16)
         g_input[x, y], g_input[x, y + 1] = result[:, :128], result[:, 128:]
         grad = jnp.concatenate(
             [td[x + 1, y + 1, 32:64, :], td[x + 1, y + 2, 32:64, :]], axis=1
@@ -585,19 +627,12 @@
     counts = tuple(lax.axis_size(axis) for axis in AXES)
     nx, ny, nz = counts
     total = nx * ny * nz
-    at_x, at_y, at_z = (lax.axis_index(axis) for axis in AXES)
     chans, depth, height, length = features.shape
     wide = w_lift.shape[0]
     scale = 1.0 / math.sqrt(total * depth * height * length)
     f32, bf16 = jnp.float32, jnp.bfloat16
     shape = jax.ShapeDtypeStruct
     params = pltpu.CompilerParams(vmem_limit_bytes=ROOMY)
-
-    def ahead(weight):
-        return weight.transpose(2, 0, 1).reshape(weight.shape[2], -1)
-
-    def back(weight):
-        return jnp.flip(weight, 0).transpose(1, 0, 2).reshape(weight.shape[1], -1)
 
     rows = jnp.concatenate([features, cotangent]).transpose(1, 2, 0, 3)
     ext = halo(rows, counts, 2)
@@ -607,18 +642,33 @@
         out_shape=(field, field, shape((16, 128), bf16)),
         in_specs=vmem(3),
         out_specs=vmem(3),
-        scratch_shapes=[pltpu.VMEM((8, 8, 192, 256), bf16), pltpu.VMEM((64, 128), f32)],
+        scratch_shapes=[
+            pltpu.VMEM((8, 8, 192, 256), bf16),
+            pltpu.VMEM((64, 128), f32),
+            pltpu.VMEM((2, chans, 27 * chans), bf16),
+        ],
         compiler_params=params,
         name="fine",
-    )(ext, ahead(w_fine_in), back(w_fine_out))
-
-    full = spread(mine, counts, False, 0)
-
-    def pick(size, parts, index):
-        each = size // parts
-        return (jnp.arange(size)[:, None] == index * each + jnp.arange(each)).astype(bf16)
-
-    at_o = at_y * nz + at_z
+    )(ext, w_fine_in, w_fine_out)
+
+    w_in9 = w_coarse_in.reshape(9, 3 * chans, wide)
+    w_mid9 = w_coarse_mid.reshape(9, 3 * wide, wide)
+    full, mid_back, in_back = spread_call(
+        lambda *refs: gather_kernel(counts, *refs),
+        counts,
+        0,
+        (
+            shape((total,) + mine.shape, bf16),
+            shape(w_mid9.shape, bf16),
+            shape((9, 3 * wide, chans), bf16),
+        ),
+        [],
+        "gather",
+        mine,
+        w_mid9,
+        w_in9,
+    )
+
     co, cw = wide // (ny * nz), wide // nx
     ci = chans // nx
     pads = [3 * chans, 3 * wide, 3 * cw, 3 * ci]
@@ -630,24 +680,14 @@
             shape((9, co, 3 * ci), f32),
             shape((chans // (ny * nz), cw), f32),
         ),
-        in_specs=vmem(11),
+        in_specs=vmem(6),
         out_specs=vmem(4),
         scratch_shapes=[pltpu.VMEM((nx + 2, ny + 2, 128, k), bf16) for k in pads]
         + [pltpu.VMEM((nx, ny, 128, 2 * chans), bf16)],
         compiler_params=params,
         name="coarse",
     )(
-        full,
-        w_coarse_in.reshape(9, 3 * chans, wide),
-        w_coarse_mid.reshape(9, 3 * wide, wide),
-        w_lift,
-        w_lift.T,
-        flipped(w_coarse_mid).reshape(9, 3 * wide, wide),
-        flipped(w_coarse_in).reshape(9, 3 * wide, chans),
-        pick(wide, nx, at_x),
-        pick(chans, nx, at_x),
-        pick(wide, ny * nz, at_o),
-        pick(chans, ny * nz, at_o),
+        full, w_in9, w_mid9, w_lift, mid_back, in_back
     )
 
     near = pltpu.VMEM((6, 6, 3 * chans, 128), bf16)
@@ -661,12 +701,26 @@
         ),
         in_specs=vmem(6),
         out_specs=vmem(3),
-        scratch_shapes=[near, near, near, pltpu.VMEM((2, 27 * chans, chans), f32)],
+        scratch_shapes=[
+            near,
+            near,
+            near,
+            pltpu.VMEM((2, 27 * chans, chans), f32),
+            pltpu.VMEM((2, chans, 27 * chans), bf16),
+        ],
         compiler_params=params,
         name="last",
-    )(ext, z_first, d_joined, grown, ahead(w_fine_out), back(w_fine_in))
-
-    sums = spread(parts, counts, True, 1).astype(f32).sum(0) * scale
+    )(ext, z_first, d_joined, grown, w_fine_out, w_fine_in)
+
+    (sums,) = spread_call(
+        lambda *refs: sum_kernel(counts, scale, *refs),
+        counts,
+        1,
+        (shape(block, f32),),
+        [pltpu.VMEM((total,) + block, bf16)],
+        "sum_parts",
+        parts,
+    )
     sums = sums.reshape(2, -1, 27, ci).transpose(0, 2, 3, 1)
 
     def owned(grad):

time: 102 us -> 95.1 us (0.932)
  local copies, waits for them, and re-layouts: 15.6 us -> 10.5 us
  other arithmetic: 4.16 us -> 0.73 us
  Pallas kernels: 81.3 us -> 82.7 us
    transpose x8 -> x0, local copies, waits for them, and re-layouts: 3.25 us -> none  [the longest x4 3.03 us: flipped(): return jnp.flip(weight, 0).transpose(0, 2, 1)]
    convert_element_type x4 -> x0, other arithmetic: 2.47 us -> none  [pick(): (jnp.arange(size)[:, None] == index * each + jnp.arange(each)).astype(bf16)]
    reshape x4 -> x1, local copies, waits for them, and re-layouts: 3.23 us -> 0.79 us  [shards(): sums = sums.reshape(2, -1, 27, ci).transpose(0, 2, 3, 1)]
    pallas_call x2, Pallas kernels: 23.3 us -> 24.5 us  [spread_call(): pl.pallas_call(kernel, out_shape=outs, in_specs=vmem(len(args)), out_spec...]
    unnamed x22 -> x12, local copies, waits for them, and re-layouts: 8.08 us -> 8.74 us
where the time goes in v1:
time: 95.1 us; the launch traced here: 94.6 us
  Pallas kernels  82.7 us (87%)
  local copies, waits for them, and re-layouts  10.5 us (11%)
    pallas_call x2, Pallas kernels, spread_call(): pl.pallas_call(kernel, out_shape=outs, in_specs=vmem(len(args)), out_spec...  24.5 us
    pallas_call x1, Pallas kernels, shards(): pl.pallas_call(fine_kernel, out_shape=(field, field, shape((16, 128), bf1...  19.3 us
    pallas_call x1, Pallas kernels, halo(): pl.pallas_call(lambda *refs: halo_kernel(counts, *refs), out_shape=jax.Sh...  13.9 us
    pallas_call x1, Pallas kernels, shards(): pl.pallas_call(lambda *refs: coarse_kernel(counts, scale, *refs), out_sha...  13.1 us
    pallas_call x1, Pallas kernels, shards(): pl.pallas_call(lambda *refs: last_kernel(counts, *refs), out_shape=(shape...  11.9 us
    unnamed x12, local copies, waits for them, and re-layouts  8.74 us

profile of v1, /device:TPU:0, one launch (start us, length us, event | category | flops | bytes accessed | tf_op | source)
XLA Modules:
  0.0 94.6 jit_solution(6212574182439661714)
XLA Ops:
  0.6 1.4 %copy.33.refs_3_ = bf16[128,32]{1,0:T(8,128)(2,1)} copy(bf16[128,32]{0,1:T(8,128)(2,1)} %param.12) | data formatting | bytes 16384 | tf_op args[5]
  2.0 0.9 copy.31
  3.0 0.9 copy.32
  3.9 0.7 maximum_bitcast_fusion.refs_0_
  4.7 13.9 %halo.1.ext.refs_0_ = bf16[8,8,64,256]{3,2,1,0:T(8,128)(2,1)} custom-call(bf16[4,4,64,128]{3,2,1,0:T(8,128)(2,1)} %maximum_bitcast_fusion.refs_0_), custom_call_target="tpu_custom_call" | custom-call | tf_op jit(solution)/shard_map/halo/pallas_call | solution.py:387
  18.6 19.3 %fine.1 = (f32[6,6,32,256]{3,2,1,0:T(8,128)}, f32[6,6,32,256]{3,2,1,0:T(8,128)}, bf16[16,128]{1,0:T(8,128)(2,1)}) custom-call(bf16[8,8,64,256]{3,2,1,0:T(8,128)(2,1)} %halo.1.ext.refs_0_, bf16[27,32,32]{2,1,0:T(8,128)(2,1)} %refs_5_.1, bf16[27,32,32]{2,1,0:T(8,128)(2,1)} %refs_4_.1), custom_call_target="tpu_custom_call" | custom-call | tf_op jit(solution)/shard_map/fine/pallas_call | solution.py:640
  37.9 13.7 %gather.1 = (bf16[32,16,128]{2,1,0:T(8,128)(2,1)}, bf16[9,384,128]{2,1,0:T(8,128)(2,1)}, bf16[9,384,32]{2,1,0:T(8,128)(2,1)}) custom-call(bf16[16,128]{1,0:T(8,128)(2,1)} %get-tuple-element.22.refs_0_, bf16[9,384,128]{2,1,0:T(8,128)(2,1)} %bitcast.19, bf16[9,96,128]{2,1,0:T(8,128)(2,1)} %bitcast.22), custom_call_target="tpu_custom_call" | custom-call | tf_op jit(solution)/shard_map/gather/pallas_call | solution.py:90
  51.6 13.1 %coarse.1 = (f32[3,3,64,256]{3,2,1,0:T(8,128)}, f32[9,16,96]{2,1,0:T(8,128)}, f32[9,16,24]{2,1,0:T(8,128)}, f32[4,32]{1,0:T(4,128)}) custom-call(bf16[32,16,128]{2,1,0:T(8,128)(2,1)} %get-tuple-element.23.refs_0_, bf16[9,96,128]{2,1,0:T(8,128)(2,1)} %bitcast.23, bf16[9,384,128]{2,1,0:T(8,128)(2,1)} %bitcast.20, bf16[128,32]{1,0:T(8,128)(2,1)} %copy.33.refs_3_, ...), custom_call_target="tpu_custom_call" | custom-call | tf_op jit(solution)/shard_map/coarse/pallas_call | solution.py:675
  64.7 0.0 copy-start.1
  64.7 11.9 %last.1 = (bf16[4,4,32,128]{3,2,1,0:T(8,128)(2,1)}, bf16[4,4,32,128]{3,2,1,0:T(8,128)(2,1)}, bf16[32,8,216]{2,1,0:T(8,128)(2,1)}) custom-call(bf16[8,8,64,256]{3,2,1,0:T(8,128)(2,1)} %halo.1.ext.refs_0_, f32[6,6,32,256]{3,2,1,0:T(8,128)} %get-tuple-element.20.refs_1_, f32[6,6,32,256]{3,2,1,0:T(8,128)} %get-tuple-element.21.refs_2_, ...), custom_call_target="tpu_custom_call" | custom-call | tf_op jit(solution)/shard_map/last/pallas_call | solution.py:695
  76.6 0.0 copy-start
  76.6 1.7 %copy.36 = bf16[32,4,4,128]{3,2,1,0:T(4,128)(2,1)} copy(bf16[32,4,4,128]{3,0,2,1:T(8,128)(2,1)} %bitcast.28) | data formatting | bytes 262144
  78.3 1.6 %copy.37 = bf16[32,4,4,128]{3,2,1,0:T(4,128)(2,1)} copy(bf16[32,4,4,128]{3,0,2,1:T(8,128)(2,1)} %bitcast.27) | data formatting | bytes 262144
  79.9 10.8 %sum_parts.1 = f32[8,216]{1,0:T(8,128)} custom-call(bf16[32,8,216]{2,1,0:T(8,128)(2,1)} %get-tuple-element.29.refs_0_), custom_call_target="tpu_custom_call" | custom-call | tf_op jit(solution)/shard_map/sum_parts/pallas_call | solution.py:90
  90.7 0.0 copy-done.1
  90.7 0.1 copy.34
  90.8 0.8 copy.39
  91.6 0.8 reshape.37
  92.4 0.7 copy.40
  93.1 0.7 copy.38
  93.8 0.0 copy-done
  93.8 0.2 reshape.40
  93.9 0.7 copy.35
  (1 shorter events, 0.0 us)
Async XLA Ops:
  64.7 26.0 %copy-start.1 = (f32[9,16,24]{2,1,0:T(8,128)S(1)}, f32[9,16,24]{2,1,0:T(8,128)}, u32[]{:S(2)}) copy-start(f32[9,16,24]{2,1,0:T(8,128)} %get-tuple-element.30) | copy-start | bytes 41476
  76.6 17.2 %copy-start = (f32[9,16,96]{2,1,0:T(8,128)S(1)}, f32[9,16,96]{2,1,0:T(8,128)}, u32[]{:S(2)}) copy-start(f32[9,16,96]{2,1,0:T(8,128)} %get-tuple-element.31) | copy-start | bytes 165892

commit v2 on v1

--- a/solution.py
+++ b/solution.py
@@ -435,6 +435,15 @@
     return jnp.concatenate([weight[26 - t] for t in range(27)], axis=1)
 
 
+def grouped(count, size, body):
+    def several(g, carry):
+        for i in range(size):
+            body(g * size + i, carry)
+        return carry
+
+    lax.fori_loop(0, count // size, several, 0)
+
+
 def fine_kernel(ext, w_in, w_out, z_ref, d_ref, mine, taps, total, ws):
     ws[0], ws[1] = ahead(w_in), back(w_out)
 
@@ -445,7 +454,7 @@
             taps[x, y, f * 96 : f * 96 + 96, :] = stacked(value)
         return carry
 
-    lax.fori_loop(0, 64, fill, 0)
+    grouped(64, 4, fill)
     total[...] = jnp.zeros_like(total)
 
     def body(r, carry):
@@ -459,7 +468,7 @@
         total[...] += own * jnp.concatenate([act, d[:, :128]])
         return carry
 
-    lax.fori_loop(0, 36, body, 0)
+    grouped(36, 6, body)
     row = lax.broadcasted_iota(jnp.int32, (32, 128), 0)
     lane = lax.broadcasted_iota(jnp.int32, (32, 128), 1)
     pick = jnp.where(lane // 4 == row, 1.0, 0.0)
@@ -584,7 +593,7 @@
         tf[x, y] = stacked(ext[x + 1, y + 1, 0:32, :].astype(jnp.float32))[:, :128]
         return carry
 
-    lax.fori_loop(0, 36, fill, 0)
+    grouped(36, 3, fill)
     sums[...] = jnp.zeros_like(sums)
 
     def body(r, carry):
@@ -611,7 +620,7 @@
         sums[1] += dot_over(pair(tf), grad, (1, 1))
         return carry
 
-    lax.fori_loop(0, 8, body, 0)
+    grouped(8, 2, body)
     ci, co = 32 // nx, 32 // (ny * nz)
     for f in range(2):
         value = sums[f].reshape(27, nx, ci, 32)

time: 95.1 us -> 85 us (0.89)
  Pallas kernels: 82.7 us -> 72.6 us
    pallas_call x1, Pallas kernels: 19.3 us -> 11.8 us  [shards(): pl.pallas_call(fine_kernel, out_shape=(field, field, shape((16, 128), bf1...]
    pallas_call x1, Pallas kernels: 11.9 us -> 9.39 us  [shards(): pl.pallas_call(lambda *refs: last_kernel(counts, *refs), out_shape=(shape...]
where the time goes in v2:
time: 85 us; the launch traced here: 84.5 us
  Pallas kernels  72.6 us (85%)
  local copies, waits for them, and re-layouts  10.5 us (12%)
    pallas_call x2, Pallas kernels, spread_call(): pl.pallas_call(kernel, out_shape=outs, in_specs=vmem(len(args)), out_spec...  24.5 us
    pallas_call x1, Pallas kernels, halo(): pl.pallas_call(lambda *refs: halo_kernel(counts, *refs), out_shape=jax.Sh...  13.9 us
    pallas_call x1, Pallas kernels, shards(): pl.pallas_call(lambda *refs: coarse_kernel(counts, scale, *refs), out_sha...  13.1 us
    pallas_call x1, Pallas kernels, shards(): pl.pallas_call(fine_kernel, out_shape=(field, field, shape((16, 128), bf1...  11.8 us
    pallas_call x1, Pallas kernels, shards(): pl.pallas_call(lambda *refs: last_kernel(counts, *refs), out_shape=(shape...  9.39 us
    unnamed x12, local copies, waits for them, and re-layouts  8.74 us

profile of v2, /device:TPU:0, one launch (start us, length us, event | category | flops | bytes accessed | tf_op | source)
XLA Modules:
  0.0 84.5 jit_solution(14606102688269683957)
XLA Ops:
  0.6 1.4 %copy.33.refs_3_ = bf16[128,32]{1,0:T(8,128)(2,1)} copy(bf16[128,32]{0,1:T(8,128)(2,1)} %param.12) | data formatting | bytes 16384 | tf_op args[5]
  2.0 0.9 %copy.31 = bf16[32,4,4,128]{3,0,2,1:T(8,128)(2,1)S(1)} copy(bf16[32,4,4,128]{3,2,1,0:T(4,128)(2,1)} %param.7) | data formatting | bytes 262144 | tf_op args[0]
  3.0 0.9 %copy.32 = bf16[32,4,4,128]{3,0,2,1:T(8,128)(2,1)S(1)} copy(bf16[32,4,4,128]{3,2,1,0:T(4,128)(2,1)} %param.8) | data formatting | bytes 262144 | tf_op args[1]
  3.9 0.7 maximum_bitcast_fusion.refs_0_
  4.7 13.9 %halo.1.ext.refs_0_ = bf16[8,8,64,256]{3,2,1,0:T(8,128)(2,1)} custom-call(bf16[4,4,64,128]{3,2,1,0:T(8,128)(2,1)} %maximum_bitcast_fusion.refs_0_), custom_call_target="tpu_custom_call" | custom-call | tf_op jit(solution)/shard_map/halo/pallas_call | solution.py:387
  18.6 11.8 %fine.1 = (f32[6,6,32,256]{3,2,1,0:T(8,128)}, f32[6,6,32,256]{3,2,1,0:T(8,128)}, bf16[16,128]{1,0:T(8,128)(2,1)}) custom-call(bf16[8,8,64,256]{3,2,1,0:T(8,128)(2,1)} %halo.1.ext.refs_0_, bf16[27,32,32]{2,1,0:T(8,128)(2,1)} %refs_5_.1, bf16[27,32,32]{2,1,0:T(8,128)(2,1)} %refs_4_.1), custom_call_target="tpu_custom_call" | custom-call | tf_op jit(solution)/shard_map/fine/pallas_call | solution.py:649
  30.3 13.7 %gather.1 = (bf16[32,16,128]{2,1,0:T(8,128)(2,1)}, bf16[9,384,128]{2,1,0:T(8,128)(2,1)}, bf16[9,384,32]{2,1,0:T(8,128)(2,1)}) custom-call(bf16[16,128]{1,0:T(8,128)(2,1)} %get-tuple-element.22.refs_0_, bf16[9,384,128]{2,1,0:T(8,128)(2,1)} %bitcast.19, bf16[9,96,128]{2,1,0:T(8,128)(2,1)} %bitcast.22), custom_call_target="tpu_custom_call" | custom-call | tf_op jit(solution)/shard_map/gather/pallas_call | solution.py:90
  44.0 13.1 %coarse.1 = (f32[3,3,64,256]{3,2,1,0:T(8,128)}, f32[9,16,96]{2,1,0:T(8,128)}, f32[9,16,24]{2,1,0:T(8,128)}, f32[4,32]{1,0:T(4,128)}) custom-call(bf16[32,16,128]{2,1,0:T(8,128)(2,1)} %get-tuple-element.23.refs_0_, bf16[9,96,128]{2,1,0:T(8,128)(2,1)} %bitcast.23, bf16[9,384,128]{2,1,0:T(8,128)(2,1)} %bitcast.20, bf16[128,32]{1,0:T(8,128)(2,1)} %copy.33.refs_3_, ...), custom_call_target="tpu_custom_call" | custom-call | tf_op jit(solution)/shard_map/coarse/pallas_call | solution.py:684
  57.1 0.0 copy-start.1
  57.1 9.4 %last.1 = (bf16[4,4,32,128]{3,2,1,0:T(8,128)(2,1)}, bf16[4,4,32,128]{3,2,1,0:T(8,128)(2,1)}, bf16[32,8,216]{2,1,0:T(8,128)(2,1)}) custom-call(bf16[8,8,64,256]{3,2,1,0:T(8,128)(2,1)} %halo.1.ext.refs_0_, f32[6,6,32,256]{3,2,1,0:T(8,128)} %get-tuple-element.20.refs_1_, f32[6,6,32,256]{3,2,1,0:T(8,128)} %get-tuple-element.21.refs_2_, ...), custom_call_target="tpu_custom_call" | custom-call | tf_op jit(solution)/shard_map/last/pallas_call | solution.py:704
  66.5 0.0 copy-start
  66.5 1.7 %copy.36 = bf16[32,4,4,128]{3,2,1,0:T(4,128)(2,1)} copy(bf16[32,4,4,128]{3,0,2,1:T(8,128)(2,1)} %bitcast.28) | data formatting | bytes 262144
  68.2 1.6 %copy.37 = bf16[32,4,4,128]{3,2,1,0:T(4,128)(2,1)} copy(bf16[32,4,4,128]{3,0,2,1:T(8,128)(2,1)} %bitcast.27) | data formatting | bytes 262144
  69.8 10.8 %sum_parts.1 = f32[8,216]{1,0:T(8,128)} custom-call(bf16[32,8,216]{2,1,0:T(8,128)(2,1)} %get-tuple-element.29.refs_0_), custom_call_target="tpu_custom_call" | custom-call | tf_op jit(solution)/shard_map/sum_parts/pallas_call | solution.py:90
  80.6 0.0 copy-done.1
  80.6 0.1 copy.34
  80.7 0.8 copy.39
  81.5 0.8 reshape.37
  82.3 0.7 copy.40
  83.0 0.7 copy.38
  83.7 0.0 copy-done
  83.7 0.2 reshape.40
  83.8 0.7 copy.35
  (1 shorter events, 0.0 us)
Async XLA Ops:
  57.1 23.5 %copy-start.1 = (f32[9,16,24]{2,1,0:T(8,128)S(1)}, f32[9,16,24]{2,1,0:T(8,128)}, u32[]{:S(2)}) copy-start(f32[9,16,24]{2,1,0:T(8,128)} %get-tuple-element.30) | copy-start | bytes 41476
  66.5 17.2 %copy-start = (f32[9,16,96]{2,1,0:T(8,128)S(1)}, f32[9,16,96]{2,1,0:T(8,128)}, u32[]{:S(2)}) copy-start(f32[9,16,96]{2,1,0:T(8,128)} %get-tuple-element.31) | copy-start | bytes 165892
